TPU v7x, 32 devices: a whole 2x2x4 slice. The times are simulated.
32 devices in a mesh: ctx: 8 (over z, core), head: 4 (over y, x).
Axes of the slice: x: 2, y: 2, z: 4, core: 2. Of those that a mesh axis runs over, the one named last changes fastest.
Arguments:
- ssd_input: bfloat16 [4096, 4096], P('ctx', 'head'), may hold values from -0.29882812 to 0.29882812
- log_decay: float32 [64, 4096], P('head', 'ctx'), may hold values from -2.5 to 0
- write_proj: bfloat16 [4096, 4, 128], P('ctx', 'head'), may hold values from -0.23925781 to 0.23925781
- read_proj: bfloat16 [4096, 4, 128], P('ctx', 'head'), may hold values from -0.23925781 to 0.23925781
- in_weight: bfloat16 [4096, 4096], P(None, 'head'), may hold values from -0.125 to 0.125
- out_weight: bfloat16 [4096, 4096], P('head'), may hold values from -0.125 to 0.125
- out_grad: bfloat16 [4096, 4096], P('ctx', 'head'), may hold values from -6 to 6
Outputs:
- input_grad: bfloat16 [4096, 4096], P('ctx', 'head')
- write_grad: float32 [4096, 4, 128], P('ctx', 'head')
- read_grad: float32 [4096, 4, 128], P('ctx', 'head')
All inputs are finite; a program needn't handle non-finite values.
Results may differ from a plain program's by a relative error of at most 0.017.
Values may be sent and summed in bfloat16 or wider, within the bound.
A program may use at most 128 MiB of HBM per device.

v0:
```python
import jax
import jax.numpy as jnp
from jax import lax
from jax.sharding import PartitionSpec as P

SPAN = 256


HIGH = lax.Precision.HIGHEST


def per_device(ssd_input, log_decay, write_proj, read_proj, in_weight, out_weight, out_grad):
    steps = ssd_input.shape[0]
    heads = log_decay.shape[0]
    width = ssd_input.shape[1]
    head_size = width // heads
    nstate = write_proj.shape[2]
    nchunk = steps // SPAN
    dy_sum = lax.dot_general(
        lax.all_gather(out_grad, "head", axis=1, tiled=True),
        out_weight,
        (((1,), (1,)), ((), ())),
        preferred_element_type=jnp.float32,
    )
    out_step = dy_sum.astype(jnp.bfloat16)
    writes = write_proj.reshape(steps, nstate)
    reads = read_proj.reshape(steps, nstate)
    stretch_cum = jnp.transpose(
        jnp.cumsum(log_decay.reshape(heads, nchunk, SPAN), axis=2), (1, 0, 2)
    )
    xs = ssd_input.reshape(nchunk, SPAN, heads, head_size)
    dys = out_step.reshape(nchunk, SPAN, heads, head_size)
    write_blocks = writes.reshape(nchunk, SPAN, nstate)
    read_blocks = reads.reshape(nchunk, SPAN, nstate)
    order = lax.broadcasted_iota(jnp.int32, (SPAN, SPAN), 0) >= lax.broadcasted_iota(
        jnp.int32, (SPAN, SPAN), 1
    )

    def head_rows(per_head):
        return jnp.repeat(per_head.T, head_size, axis=1)

    def forward_stretch(state, pieces):
        xq, dq, wq, rq, cumul = pieces
        wq_f = wq.astype(jnp.float32)
        rq_f = rq.astype(jnp.float32)
        diff = cumul[:, :, None] - cumul[:, None, :]
        decay = jnp.where(order[None], jnp.exp(jnp.where(order[None], diff, 0.0)), 0.0)
        scores = lax.dot_general(
            rq, wq, (((1,), (1,)), ((), ())), preferred_element_type=jnp.float32
        )
        mixed = jnp.einsum("thp,shp->hts", dq, xq, preferred_element_type=jnp.float32)
        weight = jnp.sum(decay * mixed, axis=0)
        read_part = jnp.dot(weight, wq_f, precision=HIGH)
        write_part = jnp.dot(weight.T, rq_f, precision=HIGH)
        dq_f = dq.astype(jnp.float32)
        input_part = jnp.einsum("hst,shp->thp", decay * scores[None], dq_f, precision=HIGH).reshape(
            SPAN, width
        )
        grown = dq_f.reshape(SPAN, width) * head_rows(jnp.exp(cumul))
        read_part = read_part + jnp.dot(grown, state, precision=HIGH)
        faded = xq.astype(jnp.float32).reshape(SPAN, width) * head_rows(
            jnp.exp(cumul[:, -1:] - cumul)
        )
        ending = jnp.dot(faded.T, wq_f, precision=HIGH)
        leaving = jnp.dot(grown.T, rq_f, precision=HIGH)
        state = jnp.repeat(jnp.exp(cumul[:, -1]), head_size)[:, None] * state + ending
        return (state, (input_part, read_part, write_part, leaving))

    zeros = jnp.zeros((width, nstate), jnp.float32)
    last_state, (input_intra, read_local, write_intra, leavings) = lax.scan(
        forward_stretch, zeros, (xs, dys, write_blocks, read_blocks, stretch_cum)
    )

    def backward_stretch(carry, pieces):
        xq, wq, cumul, leave = pieces
        fade_rows = head_rows(jnp.exp(cumul[:, -1:] - cumul))
        input_part = jnp.dot(wq.astype(jnp.float32), carry.T, precision=HIGH) * fade_rows
        write_part = jnp.dot(
            xq.astype(jnp.float32).reshape(SPAN, width) * fade_rows, carry, precision=HIGH
        )
        carry = leave + jnp.repeat(jnp.exp(cumul[:, -1]), head_size)[:, None] * carry
        return (carry, (input_part, write_part))

    first_grad, (input_inter, write_inter) = lax.scan(
        backward_stretch, zeros, (xs, write_blocks, stretch_cum, leavings), reverse=True
    )
    device_cum = jnp.cumsum(log_decay, axis=1)
    total = device_cum[:, -1]
    totals = lax.all_gather(total[None, :], "ctx", axis=0, tiled=True)
    me = lax.axis_index("ctx")
    sums = jnp.cumsum(totals, axis=0)
    mine = lax.dynamic_index_in_dim(sums, me, 0, keepdims=False)
    own = lax.dynamic_index_in_dim(totals, me, 0, keepdims=False)
    carry = (zeros, zeros)
    ends = lax.all_gather(last_state[None].astype(jnp.bfloat16), "ctx", axis=0, tiled=True).astype(
        jnp.float32
    )
    lefts = lax.all_gather(first_grad[None].astype(jnp.bfloat16), "ctx", axis=0, tiled=True).astype(
        jnp.float32
    )
    count = ends.shape[0]
    index = jnp.arange(count, dtype=jnp.int32)
    ahead = (mine - own)[None, :] - sums
    behind = sums - totals - mine[None, :]
    w_ahead = jnp.where((index < me)[:, None], jnp.exp(jnp.minimum(ahead, 0.0)), 0.0)
    w_behind = jnp.where((index > me)[:, None], jnp.exp(jnp.minimum(behind, 0.0)), 0.0)
    scale_ahead = jnp.repeat(w_ahead, head_size, axis=1)[:, :, None]
    scale_behind = jnp.repeat(w_behind, head_size, axis=1)[:, :, None]
    state_in = carry[0] + jnp.sum(scale_ahead * ends, axis=0)
    grad_in = carry[1] + jnp.sum(scale_behind * lefts, axis=0)
    grow_dev = head_rows(jnp.exp(device_cum))
    fade_dev = head_rows(jnp.exp(total[:, None] - device_cum))
    read_grad = read_local.reshape(steps, nstate) + jnp.dot(
        out_step.astype(jnp.float32) * grow_dev, state_in, precision=HIGH
    )
    write_grad = (write_intra + write_inter).reshape(steps, nstate) + jnp.dot(
        ssd_input.astype(jnp.float32) * fade_dev, grad_in, precision=HIGH
    )
    x_total = input_intra.reshape(steps, width) + input_inter.reshape(steps, width)
    x_total = x_total + jnp.dot(writes.astype(jnp.float32), grad_in.T, precision=HIGH) * fade_dev
    x_grad = x_total.astype(jnp.bfloat16)
    terms = lax.dot_general(
        x_grad, in_weight, (((1,), (1,)), ((), ())), preferred_element_type=jnp.float32
    )
    input_grad = lax.psum_scatter(
        terms.astype(jnp.bfloat16), "head", scatter_dimension=1, tiled=True
    )
    return (input_grad, write_grad.reshape(steps, 1, nstate), read_grad.reshape(steps, 1, nstate))


def solution(mesh):
    placed = (
        P("ctx", "head"),
        P("head", "ctx"),
        P("ctx", "head", None),
        P("ctx", "head", None),
        P(None, "head"),
        P("head", None),
        P("ctx", "head"),
    )
    return jax.shard_map(
        per_device,
        mesh=mesh,
        in_specs=placed,
        out_specs=(P("ctx", "head"), P("ctx", "head", None), P("ctx", "head", None)),
        check_vma=False,
    )
```

profile of v0, /device:TPU:0, one launch (start us, length us, event | category | flops | bytes accessed | tf_op | source)
XLA Modules:
  0.0 271.7 jit_solution(17569240834031199267)
XLA Ops:
  8.8 1.2 reduce-window.14
  12.0 1.1 copy.63
  13.1 52.1 %all-gather.7.cloned.1.call-done = bf16[512,4096]{1,0:T(8,128)(2,1)} async-done(((bf16[512,1024]{1,0:T(8,128)(2,1)}), bf16[512,4096]{1,0:T(8,128)(2,1)}) %all-gather.7.cloned.1.call-update) | async-done | bytes 4194320 | tf_op jit(solution)/shard_map/all_gather | solution.py:20
  65.2 9.2 %convolution_convert_fusion.1 = bf16[512,1024]{1,0:T(8,128)(2,1)S(1)} fusion(bf16[512,4096]{1,0:T(8,128)(2,1)} %all-gather.7.cloned.1.call-done, bf16[1024,4096]{1,0:T(8,128)(2,1)} %param.16), kind=kOutput, calls=%fused_computation.93 | convolution fusion | flops 4295491584 | bytes 13631488 | tf_op jit(solution)/shard_map/dot_general | solution.py:19
  74.4 2.3 reshape.170
  76.7 3.5 %copy.64 = bf16[2,256,16,64]{1,3,2,0:T(8,128)(2,1)} copy(bf16[2,256,16,64]{3,2,1,0:T(8,128)(2,1)} %reshape.170) | data formatting | bytes 2097152
  80.3 1.6 broadcast.33.clone2
  83.3 47.7 %while.40 = (s32[]{:T(128)}, f32[1024,128]{1,0:T(8,128)S(1)}, f32[2,256,1024]{2,1,0:T(8,128)}, f32[2,256,128]{2,1,0:T(8,128)}, f32[2,256,128]{2,1,0:T(8,128)}, /...) while((s32[]{:T(128)}, f32[1024,128]{1,0:T(8,128)S(1)}, ...), condition=%wide.region_4.5_spmd.clone.clone, body=%wide.region_2.4_spmd.clone.clone.sunk | while | flops 2377158656 | bytes 36409212 | solution.py:70
  84.5 2.5 convert_multiply_fusion.13
  87.0 2.8 %multiply_reduce_fusion.2 = f32[256,256]{1,0:T(8,128)S(1)} fusion(f32[16,256]{1,0:T(8,128)S(1)} %copy.107, pred[256,256]{1,0:T(8,128)(4,1)S(1)} %iota_compare_fusion.4, bf16[1,256,16,64]{1,3,2,0:T(8,128)(2,1)S(1)} %get-tuple-element.576, bf16[2,256,16,64]{1,3,2,0:T(8,128)(2,1)} %get-tuple-element.611, s32[]{:T(128)S(6)} %copy.121), kind=kOutput, calls=%fused_computation.24.clone.1 | convolution fusion | flops 139395072 | bytes 1409028 | tf_op jit(solution)/shard_map/while/body/eval_jaxpr/thp,shp->hts/dot_general | solution.py:51
  89.8 1.8 fusion.135
  91.7 3.5 %fusion.136 = f32[2,256,128]{2,1,0:T(8,128)} fusion(f32[2,256,128]{2,1,0:T(8,128)} %get-tuple-element.594, s32[]{:T(128)S(6)} %copy.121, f32[256,128]{1,0:T(8,128)} %fusion.135, f32[256,1024]{0,1:T(8,128)S(1)} %bitcast.231, bf16[256,1024]{0,1:T(8,128)(2,1)} %bitcast.235, f32[1024,128]{1,0:T(8,128)S(1)} %get-tuple-element.592, pred[]{:T(512)S(6)} %compare.7), kind=kOutput, calls=%fused_computation.40.clone.1 | convolution fusion | flops 403341312 | bytes 2359301 | tf_op jit(solution)/shard_map/while/body/eval_jaxpr/dot_general | solution.py:60
  95.4 2.1 convolution_add_fusion.4
  98.6 3.7 %fusion.134 = f32[16,64,256]{2,1,0:T(8,128)} fusion(f32[256,256]{1,0:T(8,128)S(1)} %fusion.133, f32[16,256]{1,0:T(8,128)S(1)} %copy-done.25, pred[256,256]{1,0:T(8,128)(4,1)S(1)} %copy-done.16, bf16[1,256,16,64]{1,3,2,0:T(8,128)(2,1)S(1)} %copy-done.1), kind=kOutput, calls=%fused_computation.25.clone.1 | convolution fusion | flops 809500672 | bytes 1916928 | tf_op jit(solution)/shard_map/while/body/eval_jaxpr/hst,shp->thp/dot_general | solution.py:56
  102.3 1.6 copy.108
  103.9 1.1 constant_dynamic-update-slice_fusion.2
  108.4 2.5 convert_multiply_fusion.13
  110.8 2.8 %multiply_reduce_fusion.2 = f32[256,256]{1,0:T(8,128)S(1)} fusion(f32[16,256]{1,0:T(8,128)S(1)} %copy.107, pred[256,256]{1,0:T(8,128)(4,1)S(1)} %iota_compare_fusion.4, bf16[1,256,16,64]{1,3,2,0:T(8,128)(2,1)S(1)} %get-tuple-element.576, bf16[2,256,16,64]{1,3,2,0:T(8,128)(2,1)} %get-tuple-element.611, s32[]{:T(128)S(6)} %copy.121), kind=kOutput, calls=%fused_computation.24.clone.1 | convolution fusion | flops 139395072 | bytes 1409028 | tf_op jit(solution)/shard_map/while/body/eval_jaxpr/thp,shp->hts/dot_general | solution.py:51
  113.7 1.8 fusion.135
  115.6 3.5 %fusion.136 = f32[2,256,128]{2,1,0:T(8,128)} fusion(f32[2,256,128]{2,1,0:T(8,128)} %get-tuple-element.594, s32[]{:T(128)S(6)} %copy.121, f32[256,128]{1,0:T(8,128)} %fusion.135, f32[256,1024]{0,1:T(8,128)S(1)} %bitcast.231, bf16[256,1024]{0,1:T(8,128)(2,1)} %bitcast.235, f32[1024,128]{1,0:T(8,128)S(1)} %get-tuple-element.592, pred[]{:T(512)S(6)} %compare.7), kind=kOutput, calls=%fused_computation.40.clone.1 | convolution fusion | flops 403341312 | bytes 2359301 | tf_op jit(solution)/shard_map/while/body/eval_jaxpr/dot_general | solution.py:60
  119.3 2.1 convolution_add_fusion.4
  122.4 3.7 %fusion.134 = f32[16,64,256]{2,1,0:T(8,128)} fusion(f32[256,256]{1,0:T(8,128)S(1)} %fusion.133, f32[16,256]{1,0:T(8,128)S(1)} %copy-done.25, pred[256,256]{1,0:T(8,128)(4,1)S(1)} %copy-done.16, bf16[1,256,16,64]{1,3,2,0:T(8,128)(2,1)S(1)} %copy-done.1), kind=kOutput, calls=%fused_computation.25.clone.1 | convolution fusion | flops 809500672 | bytes 1916928 | tf_op jit(solution)/shard_map/while/body/eval_jaxpr/hst,shp->thp/dot_general | solution.py:56
  126.1 1.6 copy.108
  127.8 1.1 constant_dynamic-update-slice_fusion.2
  131.0 1.6 broadcast.33.clone
  132.6 16.6 %while.39 = (s32[]{:T(128)}, f32[1024,128]{1,0:T(8,128)S(1)}, f32[2,256,1024]{2,1,0:T(8,128)}, f32[2,256,128]{2,1,0:T(8,128)S(1)}, f32[2,1024,128]{2,1,0:T(8,128...) while((s32[]{:T(128)}, f32[1024,128]{1,0:T(8,128)S(1)}, ...), condition=%wide.region_6.7_spmd.clone, body=%wide.region_5.6_spmd.clone.sunk | while | flops 806752256 | bytes 15009844 | solution.py:84
  134.7 1.1 constant_dynamic-slice_fusion.5
  135.8 1.8 fusion.116
  137.9 2.6 fusion.115
  143.0 1.1 constant_dynamic-slice_fusion.5
  144.1 1.8 fusion.116
  146.2 2.5 fusion.115
  151.6 1.1 reduce-window.16
  154.8 17.1 %all-reduce = f32[128]{0:T(128)S(1)} all-reduce(f32[128]{0:T(128)S(1)} %dynamic-update-slice), channel_id=2, replica_groups=mesh['ctx'=8,'head'=4] {'ctx'}, use_global_device_ids=true, to_apply=%add | all-reduce | flops 128 | bytes 1024
  172.4 3.3 %add.59 = f32[2,256,1024]{2,1,0:T(8,128)} add(f32[2,256,1024]{2,1,0:T(8,128)S(1)} %copy-done.4, f32[2,256,1024]{2,1,0:T(8,128)} %get-tuple-element.236) | non-fusion elementwise | flops 524288 | bytes 6291456 | tf_op jit(solution)/shard_map/add | solution.py:119
  175.7 1.9 copy.71
  177.7 1.9 all-gather.9.cloned.1.call-done
  179.5 2.5 fusion.59
  182.8 1.9 fusion.61
  184.8 9.8 %convolution_convert_fusion = bf16[512,4096]{1,0:T(8,128)(2,1)} fusion(bf16[512,1024]{0,1:T(8,128)(2,1)S(1)} %fusion.61, bf16[4096,1024]{1,0:T(8,128)(2,1)} %param.15), kind=kOutput, calls=%fused_computation.81 | convolution fusion | flops 4297064448 | bytes 13631488 | tf_op jit(solution)/shard_map/dot_general | solution.py:122
  194.6 1.2 copy-done.3
  196.2 1.6 broadcast_in_dim.128
  197.9 3.0 %copy.73 = f32[512,1024]{1,0:T(8,128)} copy(f32[512,1024]{0,1:T(8,128)} %bitcast.238) | data formatting | bytes 4194304 | tf_op jit(solution)/shard_map/reshape | solution.py:40
  200.9 8.8 %all-gather.11.cloned.1.call-done = bf16[8192,128]{1,0:T(8,128)(2,1)} async-done(((bf16[1024,128]{1,0:T(8,128)(2,1)}), bf16[8192,128]{1,0:T(8,128)(2,1)}) %all-gather.11.cloned.1.call-update) | async-done | bytes 2097168 | tf_op jit(solution)/shard_map/all_gather | solution.py:95
  209.8 2.5 fusion.58
  212.3 4.1 %convolution_add_fusion.2 = f32[512,128]{1,0:T(8,128)} fusion(f32[512,128]{1,0:T(8,128)S(1)} %bitcast.242, f32[512,1024]{0,1:T(8,128)S(1)} %bitcast_multiply_fusion, f32[1024,128]{1,0:T(8,128)S(1)} %copy-done.12), kind=kOutput, calls=%fused_computation.95 | convolution fusion | flops 805371904 | bytes 3145728 | tf_op jit(solution)/shard_map/dot_general | solution.py:116
  216.5 2.6 fusion.65
  219.0 46.2 %reduce-scatter.2.cloned.1.call-done = bf16[512,1024]{1,0:T(8,128)(2,1)} async-done(((bf16[512,4096]{1,0:T(8,128)(2,1)}), bf16[512,1024]{1,0:T(8,128)(2,1)}) %reduce-scatter.2.cloned.1.call-update) | async-done | bytes 1048592 | tf_op jit(solution)/shard_map/reduce_scatter | solution.py:125
  (175 shorter events, 25.2 us)
Async XLA Ops:
  7.2 3.9 %copy-start.23 = (bf16[512,1024]{1,0:T(8,128)(2,1)S(1)}, bf16[512,1024]{1,0:T(8,128)(2,1)}, u32[]{:S(2)}) copy-start(bf16[512,1024]{1,0:T(8,128)(2,1)} %param.11) | copy-start | bytes 3145732
  7.2 58.0 %all-gather.7.cloned.1.call-start = ((), (), s32[]{:S(2)}) async-start(), calls=%async_computation.1 | async-start | bytes 5242880 | tf_op jit(solution)/shard_map/all_gather | solution.py:20
  7.9 171.6 %all-gather.9.cloned.1.call-start = ((), (), s32[]{:S(2)}) async-start(), calls=%async_computation.3 | async-start | bytes 2359296 | tf_op jit(solution)/shard_map/all_gather | solution.py:98
  11.6 62.7 %copy-start.2 = (bf16[512,1024]{0,1:T(8,128)(2,1)}, bf16[512,1024]{0,1:T(8,128)(2,1)S(1)}, u32[]{:S(2)}) copy-start(bf16[512,1024]{0,1:T(8,128)(2,1)S(1)} %copy.60) | copy-start | bytes 3145732
  74.4 5.9 %copy-start.13 = (bf16[512,1024]{1,0:T(8,128)(2,1)}, bf16[512,1024]{1,0:T(8,128)(2,1)S(1)}, u32[]{:S(2)}) copy-start(bf16[512,1024]{1,0:T(8,128)(2,1)S(1)} %convolution_convert_fusion.1) | copy-start | bytes 3145732
  84.3 2.7 copy-start.24
  84.3 2.7 copy-start.15
  87.0 2.8 %copy-start = (bf16[1,256,16,64]{1,3,2,0:T(8,128)(2,1)}, bf16[1,256,16,64]{1,3,2,0:T(8,128)(2,1)S(1)}, u32[]{:S(2)}) copy-start(bf16[1,256,16,64]{1,3,2,0:T(8,128)(2,1)S(1)} %get-tuple-element.576) | copy-start | bytes 1572868 | tf_op jit(solution)/shard_map/while
  91.7 6.9 %copy-start.25 = (f32[16,256]{1,0:T(8,128)S(1)}, f32[16,256]{1,0:T(8,128)}, u32[]{:S(2)}) copy-start(f32[16,256]{1,0:T(8,128)} %copy-done.24) | copy-start | bytes 49156 | tf_op jit(solution)/shard_map/while
  95.2 2.3 copy-start.6
  95.2 3.3 %copy-start.1 = (bf16[1,256,16,64]{1,3,2,0:T(8,128)(2,1)S(1)}, bf16[1,256,16,64]{1,3,2,0:T(8,128)(2,1)}, u32[]{:S(2)}) copy-start(bf16[1,256,16,64]{1,3,2,0:T(8,128)(2,1)} %copy-done) | copy-start | bytes 1572868 | tf_op jit(solution)/shard_map/while
  95.2 3.3 %copy-start.16 = (pred[256,256]{1,0:T(8,128)(4,1)S(1)}, pred[256,256]{1,0:T(8,128)(4,1)}, u32[]{:S(2)}) copy-start(pred[256,256]{1,0:T(8,128)(4,1)} %copy-done.15) | copy-start | bytes 196612 | tf_op jit(solution)/shard_map/while
  102.3 2.7 copy-start.7
  103.9 1.1 copy-start.18
  103.9 1.7 copy-start.8
  105.4 0.8 copy-start.19
  106.2 1.0 copy-start.9
  108.1 2.7 copy-start.24
  108.2 2.7 copy-start.15
  110.8 2.8 %copy-start = (bf16[1,256,16,64]{1,3,2,0:T(8,128)(2,1)}, bf16[1,256,16,64]{1,3,2,0:T(8,128)(2,1)S(1)}, u32[]{:S(2)}) copy-start(bf16[1,256,16,64]{1,3,2,0:T(8,128)(2,1)S(1)} %get-tuple-element.576) | copy-start | bytes 1572868 | tf_op jit(solution)/shard_map/while
  115.5 6.9 %copy-start.25 = (f32[16,256]{1,0:T(8,128)S(1)}, f32[16,256]{1,0:T(8,128)}, u32[]{:S(2)}) copy-start(f32[16,256]{1,0:T(8,128)} %copy-done.24) | copy-start | bytes 49156 | tf_op jit(solution)/shard_map/while
  119.1 2.3 copy-start.6
  119.1 3.3 %copy-start.1 = (bf16[1,256,16,64]{1,3,2,0:T(8,128)(2,1)S(1)}, bf16[1,256,16,64]{1,3,2,0:T(8,128)(2,1)}, u32[]{:S(2)}) copy-start(bf16[1,256,16,64]{1,3,2,0:T(8,128)(2,1)} %copy-done) | copy-start | bytes 1572868 | tf_op jit(solution)/shard_map/while
  119.1 3.3 %copy-start.16 = (pred[256,256]{1,0:T(8,128)(4,1)S(1)}, pred[256,256]{1,0:T(8,128)(4,1)}, u32[]{:S(2)}) copy-start(pred[256,256]{1,0:T(8,128)(4,1)} %copy-done.15) | copy-start | bytes 196612 | tf_op jit(solution)/shard_map/while
  126.1 2.7 copy-start.7
  127.7 1.1 copy-start.18
  127.8 1.7 copy-start.8
  129.2 0.8 copy-start.19
  130.0 1.0 copy-start.9
  137.9 2.7 %copy-start.10 = (f32[2,1024,128]{2,1,0:T(8,128)S(1)}, f32[2,1024,128]{2,1,0:T(8,128)}, u32[]{:S(2)}) copy-start(f32[2,1024,128]{2,1,0:T(8,128)} %get-tuple-element.641) | copy-start | bytes 3145732 | tf_op jit(solution)/shard_map/while
  146.2 2.7 copy-start.10
  149.2 26.5 %copy-start.21 = (f32[2,256,128]{2,1,0:T(8,128)}, f32[2,256,128]{2,1,0:T(8,128)S(1)}, u32[]{:S(2)}) copy-start(f32[2,256,128]{2,1,0:T(8,128)S(1)} %get-tuple-element.239) | copy-start | bytes 786436
  149.2 3.8 %copy-start.26 = (u32[32]{0:T(128)S(1)}, u32[32]{0:T(128)}, u32[]{:S(2)}) copy-start(u32[32]{0:T(128)} %constant.96) | copy-start | bytes 388
  149.2 23.2 %copy-start.4 = (f32[2,256,1024]{2,1,0:T(8,128)S(1)}, f32[2,256,1024]{2,1,0:T(8,128)}, u32[]{:S(2)}) copy-start(f32[2,256,1024]{2,1,0:T(8,128)} %get-tuple-element.234) | copy-start | bytes 6291460
  150.0 59.8 %all-gather.11.cloned.1.call-start = ((), (), s32[]{:S(2)}) async-start(), calls=%async_computation.4 | async-start | bytes 2359296 | tf_op jit(solution)/shard_map/all_gather | solution.py:95
  150.8 114.4 %reduce-scatter.2.cloned.1.call-start = ((), (), s32[]{:S(2)}) async-start(), calls=%async_computation.2 | async-start | bytes 5242880 | tf_op jit(solution)/shard_map/reduce_scatter | solution.py:125
  182.0 0.8 copy-start.11
  194.6 1.2 copy-start.3
  197.9 3.0 %copy-start.20 = (f32[2,256,128]{2,1,0:T(8,128)S(1)}, f32[2,256,128]{2,1,0:T(8,128)}, u32[]{:S(2)}) copy-start(f32[2,256,128]{2,1,0:T(8,128)} %get-tuple-element.238) | copy-start | bytes 786436
  197.9 3.0 %copy-start.22 = (f32[2,256,128]{2,1,0:T(8,128)S(1)}, f32[2,256,128]{2,1,0:T(8,128)}, u32[]{:S(2)}) copy-start(f32[2,256,128]{2,1,0:T(8,128)} %copy-done.21) | copy-start | bytes 786436
  200.9 11.4 %copy-start.12 = (f32[1024,128]{1,0:T(8,128)S(1)}, f32[1024,128]{1,0:T(8,128)}, u32[]{:S(2)}) copy-start(f32[1024,128]{1,0:T(8,128)} %copy-done.11) | copy-start | bytes 1572868
  209.7 6.7 %copy-start.17 = (f32[2,256,128]{2,1,0:T(8,128)S(1)}, f32[2,256,128]{2,1,0:T(8,128)}, u32[]{:S(2)}) copy-start(f32[2,256,128]{2,1,0:T(8,128)} %get-tuple-element.240) | copy-start | bytes 786436
  212.3 4.2 %copy-start.5 = (f32[512,1024]{1,0:T(8,128)S(1)}, f32[512,1024]{1,0:T(8,128)}, u32[]{:S(2)}) copy-start(f32[512,1024]{1,0:T(8,128)} %copy.73) | copy-start | bytes 6291460
  212.3 4.2 %copy-start.14 = (bf16[512,1024]{1,0:T(8,128)(2,1)S(1)}, bf16[512,1024]{1,0:T(8,128)(2,1)}, u32[]{:S(2)}) copy-start(bf16[512,1024]{1,0:T(8,128)(2,1)} %copy-done.13) | copy-start | bytes 3145732
Sparse Core Ops, SparseCore 0:
  9.8 55.2 all-gather.6
  150.1 29.3 all-gather.8
  181.1 28.5 all-gather.10
  213.1 51.9 reduce-scatter.1
where the time goes:
time: 273 us; the launch traced here: 272 us
  waiting for transfers between devices  110 us (40%)
  matrix products  68.2 us (25%)
  local copies, waits for them, and re-layouts  41.1 us (15%)
  other arithmetic  20.3 us (7%)
  blocking collectives  17.1 us (6%)
  between operations  14.7 us (5%)
    all_gather x1, waiting for transfers between devices, per_device(): lax.all_gather(out_grad, 'head', axis=1, tiled=True)  52.1 us
    reduce_scatter x1, waiting for transfers between devices, per_device(): lax.psum_scatter(terms.astype(jnp.bfloat16), 'head', scatter_dimension=1,...  46.2 us
    unnamed x1, blocking collectives  17.1 us
    dot_general x1, matrix products, per_device(): lax.dot_general(x_grad, in_weight, (((1,), (1,)), ((), ())), preferred_el...  9.79 us
    dot_general x1, matrix products, per_device(): lax.dot_general(lax.all_gather(out_grad, 'head', axis=1, tiled=True), out...  9.18 us
    unnamed x35, local copies, waits for them, and re-layouts  9.04 us
    all_gather x1, waiting for transfers between devices, per_device(): lax.all_gather(last_state[None].astype(jnp.bfloat16), 'ctx', axis=0, tile...  8.8 us
    dot_general x2, matrix products, forward_stretch(): jnp.einsum('hst,shp->thp', decay * scores[None], dq_f, precision=HIGH)  7.41 us
  transfers between devices with their start and end apart: 4, of which 4 were waited for; matrix products, arithmetic and copies ran while one was open for 16% of the time, Pallas kernels for 0%

commit v1 on v0

v1 whole, which is shorter than its diff:
```python
import functools

import jax
import jax.numpy as jnp
from jax import lax
from jax.experimental import pallas as pl
from jax.experimental.pallas import tpu as pltpu
from jax.sharding import PartitionSpec as P

CHUNK = 128
SUB = 2
MESH = pl.DeviceIdType.MESH
HIGH = lax.Precision.HIGHEST
F32 = jnp.float32
BF16 = jnp.bfloat16
NT = (((1,), (1,)), ((), ()))
TN = (((0,), (0,)), ((), ()))
VMEM_LIMIT = 60 * 1024 * 1024


def mm(a, b, dims=(((1,), (0,)), ((), ())), precision=None):
    return lax.dot_general(a, b, dims, precision=precision, preferred_element_type=F32)


def ring_index(place, n):
    half = n // 2
    return jnp.where(place < half, place, n + half - 1 - place)


def greet(axis, targets):
    barrier = pltpu.get_barrier_semaphore()
    for target in targets:
        pl.semaphore_signal(barrier, inc=1, device_id={axis: target}, device_id_type=MESH)
    pl.semaphore_wait(barrier, len(targets))


def gather_kernel(n, x_ref, w_ref, dy_ref, buf, wv, acc, wsem, ssem, rsem):
    rows, feats = x_ref.shape
    width = w_ref.shape[0]
    me = lax.axis_index("head")
    place = ring_index(me, n)
    right = ring_index(lax.rem(place + 1, n), n)
    left = ring_index(lax.rem(place + n - 1, n), n)
    half = rows // 2
    piece = half // SUB
    greet("head", (left, right))

    def span(d, g):
        return pl.ds(d * half + g * piece, piece)

    def copy(s, d, g):
        src = x_ref.at[span(d, g)] if s == 0 else buf.at[s - 1, span(d, g)]
        return pltpu.make_async_remote_copy(
            src_ref=src,
            dst_ref=buf.at[s, span(d, g)],
            send_sem=ssem.at[s, d, g],
            recv_sem=rsem.at[s, d, g],
            device_id={"head": right if d == 0 else left},
            device_id_type=MESH,
        )

    def owner(s, d):
        return ring_index(lax.rem(place + (n - s if d == 0 else s), n), n)

    for g in range(SUB):
        for d in range(2):
            copy(0, d, g).start()

    def weight(b):
        at = pl.multiple_of(b * feats, 128)
        return pltpu.make_async_copy(w_ref.at[:, pl.ds(at, feats)], wv.at[b], wsem.at[b])

    for b in range(n):
        weight(b).start()
    for b in range(n):
        weight(b).wait()

    tile = 256

    def accumulate(s, d, row0, count):
        own = owner(s, d)
        src = x_ref if s == 0 else buf.at[s - 1]

        @pl.loop(0, width // tile)
        def _(j):
            cols = pl.ds(pl.multiple_of(j * tile, tile), tile)
            part = mm(src[pl.ds(row0, count), :], wv[own, cols, :], NT)
            at = (pl.ds(row0, count), cols)
            if s == 0:
                acc[at] = part
            elif s == n - 1:
                dy_ref[at] = (acc[at] + part).astype(dy_ref.dtype)
            else:
                acc[at] += part

    for s in range(n - 1):
        if s > 0:
            for g in range(SUB):
                for d in range(2):
                    copy(s - 1, d, g).wait_recv()
                    copy(s, d, g).start()
        for d in range(2):
            accumulate(s, d, d * half, half)
    for g in range(SUB):
        for d in range(2):
            copy(n - 2, d, g).wait_recv()
            accumulate(n - 1, d, d * half + g * piece, piece)
    for s in range(n - 1):
        for g in range(SUB):
            for d in range(2):
                copy(s, d, g).wait_send()


def gather_product(n, grad, weight):
    rows, feats = grad.shape
    width = weight.shape[0]
    return pl.pallas_call(
        functools.partial(gather_kernel, n),
        name="gather_product",
        out_shape=jax.ShapeDtypeStruct((rows, width), BF16),
        in_specs=[
            pl.BlockSpec(memory_space=pltpu.VMEM),
            pl.BlockSpec(memory_space=pl.ANY),
        ],
        out_specs=pl.BlockSpec(memory_space=pltpu.VMEM),
        scratch_shapes=[
            pltpu.VMEM((n - 1, rows, feats), BF16),
            pltpu.VMEM((n, width, feats), BF16),
            pltpu.VMEM((rows, width), F32),
            pltpu.SemaphoreType.DMA((n,)),
            pltpu.SemaphoreType.DMA((n - 1, 2, SUB)),
            pltpu.SemaphoreType.DMA((n - 1, 2, SUB)),
        ],
        compiler_params=pltpu.CompilerParams(
            collective_id=0, has_side_effects=True, vmem_limit_bytes=VMEM_LIMIT
        ),
    )(grad, weight)


def scatter_kernel(n, x_ref, w_ref, out_ref, wv, rbuf, sbuf, wsem, ssem, rsem):
    rows, depth = x_ref.shape
    cols = out_ref.shape[1]
    me = lax.axis_index("head")
    place = ring_index(me, n)
    right = ring_index(lax.rem(place + 1, n), n)
    left = ring_index(lax.rem(place + n - 1, n), n)
    half = rows // 2
    piece = half // SUB

    def weight(b):
        return pltpu.make_async_copy(w_ref.at[pl.ds(b * cols, cols)], wv.at[b], wsem.at[b])

    for b in range(n):
        weight(b).start()
    greet("head", (left, right))
    for b in range(n):
        weight(b).wait()

    def copy(s, d, g):
        at = pl.ds(d * half + g * piece, piece)
        return pltpu.make_async_remote_copy(
            src_ref=sbuf.at[s, at],
            dst_ref=rbuf.at[s, at],
            send_sem=ssem.at[s, d, g],
            recv_sem=rsem.at[s, d, g],
            device_id={"head": right if d == 0 else left},
            device_id_type=MESH,
        )

    tile = 256

    def term(s, d, g):
        if d == 0:
            dest = ring_index(lax.rem(place + 2 * n - 1 - s, n), n)
        else:
            dest = ring_index(lax.rem(place + 1 + s, n), n)
        at = pl.ds(d * half + g * piece, piece)

        @pl.loop(0, cols // tile)
        def _(j):
            lanes = pl.ds(pl.multiple_of(j * tile, tile), tile)
            part = mm(x_ref[at, :], wv[dest, lanes, :], NT)
            if s > 0:
                part = part + rbuf[s - 1, at, lanes].astype(F32)
            if s == n - 1:
                out_ref[at, lanes] = part.astype(out_ref.dtype)
            else:
                sbuf[s, at, lanes] = part.astype(BF16)

    for s in range(n):
        for g in range(SUB):
            for d in range(2):
                if s > 0:
                    copy(s - 1, d, g).wait_recv()
                term(s, d, g)
                if s < n - 1:
                    copy(s, d, g).start()
    for s in range(n - 1):
        for g in range(SUB):
            for d in range(2):
                copy(s, d, g).wait_send()


def product_scatter(n, x_grad, weight):
    rows, depth = x_grad.shape
    cols = weight.shape[0] // n
    return pl.pallas_call(
        functools.partial(scatter_kernel, n),
        name="product_scatter",
        out_shape=jax.ShapeDtypeStruct((rows, cols), BF16),
        in_specs=[
            pl.BlockSpec(memory_space=pltpu.VMEM),
            pl.BlockSpec(memory_space=pl.ANY),
        ],
        out_specs=pl.BlockSpec(memory_space=pltpu.VMEM),
        scratch_shapes=[
            pltpu.VMEM((n, cols, depth), BF16),
            pltpu.VMEM((n - 1, rows, cols), BF16),
            pltpu.VMEM((n - 1, rows, cols), BF16),
            pltpu.SemaphoreType.DMA((n,)),
            pltpu.SemaphoreType.DMA((n - 1, 2, SUB)),
            pltpu.SemaphoreType.DMA((n - 1, 2, SUB)),
        ],
        compiler_params=pltpu.CompilerParams(
            collective_id=1, has_side_effects=True, vmem_limit_bytes=VMEM_LIMIT
        ),
    )(x_grad, weight)


PIECES = 4
POINTS = 2


def state_kernel(
    n, x_ref, ld_ref, b_ref, c_ref, dy_ref, xg_ref, wg_ref, rg_ref,
    ends, leaves, grown, faded, fades, intra, lrow, lcol, etot, wacc,
    end_own, leave_own, s_in, s_out, g_in, g_out, sem_ss, sem_sr, sem_gs, sem_gr,
):
    rows, width = x_ref.shape
    heads = ld_ref.shape[0]
    nstate = b_ref.shape[1]
    hp = width // heads
    q = CHUNK
    nc = rows // q
    pairs = heads // 2
    me = lax.axis_index("ctx")
    ahead = jnp.minimum(me + 1, n - 1)
    behind = jnp.maximum(me - 1, 0)

    barrier = pltpu.get_barrier_semaphore()

    @pl.when(me < n - 1)
    def _():
        pl.semaphore_signal(barrier, inc=1, device_id={"ctx": ahead}, device_id_type=MESH)

    @pl.when(me > 0)
    def _():
        pl.semaphore_signal(barrier, inc=1, device_id={"ctx": behind}, device_id_type=MESH)

    pl.semaphore_wait(barrier, jnp.where(me > 0, 1, 0) + jnp.where(me < n - 1, 1, 0))

    @pl.when(me == 0)
    def _():
        s_in[...] = jnp.zeros_like(s_in)

    @pl.when(me == n - 1)
    def _():
        g_in[...] = jnp.zeros_like(g_in)

    first = lax.broadcasted_iota(jnp.int32, (q, q), 0)
    second = lax.broadcasted_iota(jnp.int32, (q, q), 1)
    upto = (first <= second).astype(F32)
    downto = (first >= second).astype(F32)
    after = (first < second).astype(F32)
    ones = jnp.ones((q, nstate), F32)
    head_at = lax.broadcasted_iota(jnp.int32, (heads, width), 0) * hp
    lane_at = lax.broadcasted_iota(jnp.int32, (heads, width), 1)
    spread = ((lane_at >= head_at) & (lane_at < head_at + hp)).astype(BF16)

    def scaled(factor, state):
        out = factor[:, None, :] * state.reshape(heads, hp, nstate)
        return out.reshape(width, nstate)

    total = jnp.zeros((heads, nstate), F32)
    for k in range(nc):
        at = pl.ds(k * q, q)
        ldk = ld_ref[:, k * q : (k + 1) * q]
        lrow[k] = mm(ldk, upto, precision=HIGH)
        cols = mm(downto, ldk, NT, HIGH)
        lcol[k] = cols
        whole = mm(ldk, ones, precision=HIGH)
        total = total + whole
        etot[k] = jnp.exp(whole)
        fade = mm(jnp.exp(mm(after, ldk, NT, HIGH)).astype(BF16), spread)
        grow = mm(jnp.exp(cols).astype(BF16), spread)
        fades[at, :] = fade.astype(BF16)
        fx = (x_ref[at, :].astype(F32) * fade).astype(BF16)
        faded[at, :] = fx
        ends[k] = mm(fx, b_ref[at, :], TN)
        gd = (dy_ref[at, :].astype(F32) * grow).astype(BF16)
        grown[at, :] = gd
        leaves[k] = mm(gd, c_ref[at, :], TN)
    etot[nc] = jnp.exp(total)

    state = ends[0]
    for k in range(1, nc):
        state = scaled(etot[k], state) + ends[k]
    end_own[...] = state
    grad = leaves[nc - 1]
    for k in range(nc - 2, -1, -1):
        grad = leaves[k] + scaled(etot[k], grad)
    leave_own[...] = grad

    hstep = heads // PIECES
    step = width // PIECES

    def relay(own, got, out, sends, recvs, target, receives, passes):
        def copy(i):
            at = pl.ds(i * step, step)
            return pltpu.make_async_remote_copy(
                src_ref=out.at[at],
                dst_ref=got.at[at],
                send_sem=sends.at[i],
                recv_sem=recvs.at[i],
                device_id={"ctx": target},
                device_id_type=MESH,
            )

        def run():
            for i in range(PIECES):
                at = pl.ds(i * step, step)

                @pl.when(receives)
                def _():
                    copy(i).wait_recv()

                @pl.when(passes)
                def _():
                    factor = etot[nc, i * hstep : (i + 1) * hstep, :]
                    come = got[at, :].astype(F32).reshape(hstep, hp, nstate)
                    come = (factor[:, None, :] * come).reshape(step, nstate)
                    out[at, :] = (own[at, :] + come).astype(BF16)
                    copy(i).start()

        def finish():
            @pl.when(passes)
            def _():
                for i in range(PIECES):
                    copy(i).wait_send()

        return run, finish

    run_s, finish_s = relay(end_own, s_in, s_out, sem_ss, sem_sr, ahead, me > 0, me < n - 1)
    run_g, finish_g = relay(leave_own, g_in, g_out, sem_gs, sem_gr, behind, me < n - 1, me > 0)
    points = POINTS * nc
    at_s = (me * points) // n
    at_g = ((n - 1 - me) * points) // n

    low = lax.broadcasted_iota(jnp.int32, (q, 2 * hp), 1) < hp
    keep = jnp.concatenate([first <= second, first <= second], axis=1)

    @pl.loop(0, nc)
    def _(k):
        at = pl.ds(pl.multiple_of(k * q, q), q)
        bk = b_ref[at, :]
        ck = c_ref[at, :]
        score = mm(bk, ck, NT)
        score2 = jnp.concatenate([score, score], axis=1)
        colk = lcol[k]
        for j in range(pairs):
            if j % (pairs // POINTS) == 0:
                point = k * POINTS + j // (pairs // POINTS)
                pl.when(point == at_s)(run_s)
                pl.when(point == at_g)(run_g)
            lanes = slice(j * 2 * hp, (j + 1) * 2 * hp)
            dyp = dy_ref[at, lanes]
            none = jnp.zeros_like(dyp)
            dyst = jnp.concatenate([jnp.where(low, dyp, none), jnp.where(low, none, dyp)], axis=0)
            mixed = mm(x_ref[at, lanes], dyst, NT)
            d0 = lrow[k, 2 * j : 2 * j + 1, :] - colk[:, 2 * j : 2 * j + 1]
            d1 = lrow[k, 2 * j + 1 : 2 * j + 2, :] - colk[:, 2 * j + 1 : 2 * j + 2]
            decay = jnp.exp(jnp.where(keep, jnp.concatenate([d0, d1], axis=1), -1e30))
            if j == 0:
                wacc[...] = decay * mixed
            else:
                wacc[...] += decay * mixed
            intra[at, lanes] = mm((decay * score2).astype(BF16), dyst)
        both = wacc[...]
        weight = (both[:, :q] + both[:, q:]).astype(BF16)
        wg_ref[at, :] = mm(weight, ck)
        rg_ref[at, :] = mm(weight, bk, TN)

    state = s_in[...].astype(F32)
    for k in range(nc):
        at = pl.ds(k * q, q)
        rg_ref[at, :] += mm(grown[at, :], state.astype(BF16))
        if k < nc - 1:
            state = scaled(etot[k], state) + ends[k]
    grad = g_in[...].astype(F32)
    for k in range(nc - 1, -1, -1):
        at = pl.ds(k * q, q)
        gb = grad.astype(BF16)
        inter = mm(b_ref[at, :], gb, NT)
        xg_ref[at, :] = (intra[at, :] + fades[at, :].astype(F32) * inter).astype(BF16)
        wg_ref[at, :] += mm(faded[at, :], gb)
        if k > 0:
            grad = leaves[k] + scaled(etot[k], grad)
    finish_s()
    finish_g()


def state_part(n, x, log_decay, writes, reads, dy):
    rows, width = x.shape
    heads = log_decay.shape[0]
    nstate = writes.shape[1]
    nc = rows // CHUNK
    vm = pl.BlockSpec(memory_space=pltpu.VMEM)
    return pl.pallas_call(
        functools.partial(state_kernel, n),
        name="state_part",
        out_shape=(
            jax.ShapeDtypeStruct((rows, width), BF16),
            jax.ShapeDtypeStruct((rows, nstate), F32),
            jax.ShapeDtypeStruct((rows, nstate), F32),
        ),
        in_specs=[vm] * 5,
        out_specs=(vm, vm, vm),
        scratch_shapes=[
            pltpu.VMEM((nc, width, nstate), F32),
            pltpu.VMEM((nc, width, nstate), F32),
            pltpu.VMEM((rows, width), BF16),
            pltpu.VMEM((rows, width), BF16),
            pltpu.VMEM((rows, width), BF16),
            pltpu.VMEM((rows, width), F32),
            pltpu.VMEM((nc, heads, CHUNK), F32),
            pltpu.VMEM((nc, CHUNK, heads), F32),
            pltpu.VMEM((nc + 1, heads, nstate), F32),
            pltpu.VMEM((CHUNK, 2 * CHUNK), F32),
            pltpu.VMEM((width, nstate), F32),
            pltpu.VMEM((width, nstate), F32),
            pltpu.VMEM((width, nstate), BF16),
            pltpu.VMEM((width, nstate), BF16),
            pltpu.VMEM((width, nstate), BF16),
            pltpu.VMEM((width, nstate), BF16),
            pltpu.SemaphoreType.DMA((PIECES,)),
            pltpu.SemaphoreType.DMA((PIECES,)),
            pltpu.SemaphoreType.DMA((PIECES,)),
            pltpu.SemaphoreType.DMA((PIECES,)),
        ],
        compiler_params=pltpu.CompilerParams(
            collective_id=2, has_side_effects=True, vmem_limit_bytes=VMEM_LIMIT
        ),
    )(x, log_decay, writes, reads, dy)


def per_device(
    nctx, nhead, ssd_input, log_decay, write_proj, read_proj, in_weight, out_weight, out_grad
):
    steps = ssd_input.shape[0]
    nstate = write_proj.shape[2]
    dy = gather_product(nhead, out_grad, out_weight)
    x_grad, write_grad, read_grad = state_part(
        nctx,
        ssd_input,
        log_decay,
        write_proj.reshape(steps, nstate),
        read_proj.reshape(steps, nstate),
        dy,
    )
    input_grad = product_scatter(nhead, x_grad, in_weight)
    return (input_grad, write_grad.reshape(steps, 1, nstate), read_grad.reshape(steps, 1, nstate))


def solution(mesh):
    placed = (
        P("ctx", "head"),
        P("head", "ctx"),
        P("ctx", "head", None),
        P("ctx", "head", None),
        P(None, "head"),
        P("head", None),
        P("ctx", "head"),
    )
    return jax.shard_map(
        functools.partial(per_device, mesh.shape["ctx"], mesh.shape["head"]),
        mesh=mesh,
        in_specs=placed,
        out_specs=(P("ctx", "head"), P("ctx", "head", None), P("ctx", "head", None)),
        check_vma=False,
    )
```

time: 273 us -> 118 us (0.43)
  Pallas kernels: 0 us -> 113 us
  waiting for transfers between devices: 110 us -> 0 us
  matrix products: 68.2 us -> 0 us
  local copies, waits for them, and re-layouts: 41.1 us -> 3.68 us
  other arithmetic: 20.3 us -> 0 us
  blocking collectives: 17.1 us -> 0 us
  between operations: 14.7 us -> 0.67 us
    pallas_call x0 -> x3, Pallas kernels: none -> 113 us  [the longest x1 44.5 us: product_scatter(): pl.pallas_call(functools.partial(scatter_kernel, n), name='product_scatte...]
    dot_general x25 -> x0, matrix products: 68.2 us -> none  [the longest x1 9.79 us: per_device(): lax.dot_general(x_grad, in_weight, (((1,), (1,)), ((), ())), preferred_el...]
    all_gather x3 -> x0, waiting for transfers between devices: 62.7 us -> none  [the longest x1 52.1 us: per_device(): lax.all_gather(out_grad, 'head', axis=1, tiled=True)]
    reduce_scatter x1 -> x0, waiting for transfers between devices: 46.2 us -> none  [per_device(): lax.psum_scatter(terms.astype(jnp.bfloat16), 'head', scatter_dimension=1,...]
    unnamed x1 -> x0, blocking collectives: 17.1 us -> none
    reshape x7 -> x0, local copies, waits for them, and re-layouts: 7.09 us -> none  [the longest x3 3.68 us: head_rows(): return jnp.repeat(per_head.T, head_size, axis=1)]
    another operation x10 -> x0, local copies, waits for them, and re-layouts: 5.58 us -> none
    unnamed x35 -> x7, local copies, waits for them, and re-layouts: 9.04 us -> 3.68 us
  transfers between devices with their start and end apart: 4 -> 0, of which waited for: 4 -> 0; matrix products, arithmetic and copies ran while one was open for 16% -> 0% of each run, Pallas kernels for 0% -> 0%
where the time goes in v1:
time: 118 us; the launch traced here: 117 us
  Pallas kernels  113 us (96%)
  local copies, waits for them, and re-layouts  3.68 us (3%)
    pallas_call x1, Pallas kernels, product_scatter(): pl.pallas_call(functools.partial(scatter_kernel, n), name='product_scatte...  44.5 us
    pallas_call x1, Pallas kernels, gather_product(): pl.pallas_call(functools.partial(gather_kernel, n), name='gather_product'...  43.6 us
    pallas_call x1, Pallas kernels, state_part(): pl.pallas_call(functools.partial(state_kernel, n), name='state_part', out...  24.9 us
    unnamed x7, local copies, waits for them, and re-layouts  3.68 us

profile of v1, /device:TPU:0, one launch (start us, length us, event | category | flops | bytes accessed | tf_op | source)
XLA Modules:
  0.0 117.4 jit_solution(2520279481150391899)
XLA Ops:
  0.6 43.6 %gather_product.1.dy_ref = bf16[512,1024]{1,0:T(8,128)(2,1)} custom-call(bf16[512,1024]{1,0:T(8,128)(2,1)} %x_ref.2, bf16[1024,4096]{1,0:T(8,128)(2,1)} %w_ref.2), custom_call_target="tpu_custom_call" | custom-call | tf_op jit(solution)/shard_map/gather_product/pallas_call | solution.py:117
  44.2 24.9 %state_part.1 = (bf16[512,1024]{1,0:T(8,128)(2,1)}, f32[512,128]{1,0:T(8,128)}, f32[512,128]{1,0:T(8,128)}) custom-call(bf16[512,1024]{1,0:T(8,128)(2,1)} %x_ref.3, f32[16,512]{1,0:T(8,128)} %ld_ref.1, bf16[512,128]{1,0:T(8,128)(2,1)} %bitcast.10, bf16[512,128]{1,0:T(8,128)(2,1)} %bitcast.11, bf16[512,1024]{1,0:T(8,128)(2,1)} %gather_product.1.dy_ref), custom_call_target="tpu_custom_call" | custom-call | tf_op jit(solution)/shard_map/state_part/pallas_call | solution.py:418
  69.1 0.0 copy-start.1
  69.1 0.0 copy-start
  69.1 44.5 %product_scatter.1 = bf16[512,1024]{1,0:T(8,128)(2,1)} custom-call(bf16[512,1024]{1,0:T(8,128)(2,1)} %get-tuple-element.6.x_ref, bf16[4096,1024]{1,0:T(8,128)(2,1)} %w_ref.3), custom_call_target="tpu_custom_call" | custom-call | tf_op jit(solution)/shard_map/product_scatter/pallas_call | solution.py:207
  113.7 2.3 %copy.15 = bf16[512,1024]{1,0:T(8,128)(2,1)} copy(bf16[512,1024]{1,0:T(8,128)(2,1)} %product_scatter.1) | data formatting | bytes 2097152
  115.9 0.0 copy-done.1
  115.9 0.7 copy.16
  116.6 0.0 copy-done
  116.6 0.7 copy.17
Async XLA Ops:
  69.1 46.8 %copy-start.1 = (f32[512,128]{1,0:T(8,128)S(1)}, f32[512,128]{1,0:T(8,128)}, u32[]{:S(2)}) copy-start(f32[512,128]{1,0:T(8,128)} %get-tuple-element.7) | copy-start | bytes 786436
  69.1 47.5 %copy-start = (f32[512,128]{1,0:T(8,128)S(1)}, f32[512,128]{1,0:T(8,128)}, u32[]{:S(2)}) copy-start(f32[512,128]{1,0:T(8,128)} %get-tuple-element.8) | copy-start | bytes 786436

commit v2 on v0

v2 whole, which is shorter than its diff:
```python
import functools

import jax
import jax.numpy as jnp
from jax import lax
from jax.experimental import pallas as pl
from jax.experimental.pallas import tpu as pltpu
from jax.sharding import PartitionSpec as P

CHUNK = 128
SUB = 2
PIECES = 4
POINTS = 2
TILE = 256
MESH = pl.DeviceIdType.MESH
HIGH = lax.Precision.HIGHEST
F32 = jnp.float32
BF16 = jnp.bfloat16
NT = (((1,), (1,)), ((), ()))
TN = (((0,), (0,)), ((), ()))
VMEM_LIMIT = 60 * 1024 * 1024


def mm(a, b, dims=(((1,), (0,)), ((), ())), precision=None):
    return lax.dot_general(a, b, dims, precision=precision, preferred_element_type=F32)


def ring_index(place, n):
    half = n // 2
    return jnp.where(place < half, place, n + half - 1 - place)


def layer_kernel(
    nctx, nhead, grad_ref, x_hbm, ld_ref, b_ref, c_ref, wo_hbm, wi_hbm,
    out_ref, wg_ref, rg_ref,
    xv, dy, xg, wo, wi, acc, gbuf, rbuf, sbuf,
    ends, leaves, grown, faded, fades, grows, intra, decays, mixes, lrow, lcol, etot, wacc,
    end_own, leave_own, s_in, s_out, g_in, g_out,
    x_sem, wo_sem, wi_sem, ag_ss, ag_sr, rs_ss, rs_sr, st_ss, st_sr, gr_ss, gr_sr,
):
    rows, feats = grad_ref.shape
    heads = ld_ref.shape[0]
    width = wo.shape[1]
    cols = out_ref.shape[1]
    nstate = b_ref.shape[1]
    hp = width // heads
    q = CHUNK
    nc = rows // q
    pairs = heads // 2
    n = nhead
    half = rows // 2
    piece = half // SUB

    def x_copy():
        return pltpu.make_async_copy(x_hbm, xv, x_sem)

    def wo_copy(b):
        at = pl.multiple_of(b * feats, 128)
        return pltpu.make_async_copy(wo_hbm.at[:, pl.ds(at, feats)], wo.at[b], wo_sem.at[b])

    def wi_copy(b):
        return pltpu.make_async_copy(wi_hbm.at[pl.ds(b * cols, cols)], wi.at[b], wi_sem.at[b])

    x_copy().start()
    for b in range(n):
        wo_copy(b).start()

    me = lax.axis_index("head")
    place = ring_index(me, n)
    right = ring_index(lax.rem(place + 1, n), n)
    left = ring_index(lax.rem(place + n - 1, n), n)
    ctx = lax.axis_index("ctx")
    ahead = jnp.minimum(ctx + 1, nctx - 1)
    behind = jnp.maximum(ctx - 1, 0)

    barrier = pltpu.get_barrier_semaphore()
    for target in (left, right):
        pl.semaphore_signal(barrier, inc=1, device_id={"head": target}, device_id_type=MESH)

    @pl.when(ctx < nctx - 1)
    def _():
        pl.semaphore_signal(barrier, inc=1, device_id={"ctx": ahead}, device_id_type=MESH)

    @pl.when(ctx > 0)
    def _():
        pl.semaphore_signal(barrier, inc=1, device_id={"ctx": behind}, device_id_type=MESH)

    pl.semaphore_wait(
        barrier, 2 + jnp.where(ctx > 0, 1, 0) + jnp.where(ctx < nctx - 1, 1, 0)
    )

    def span(d, g):
        return pl.ds(d * half + g * piece, piece)

    def ag_copy(s, d, g):
        src = grad_ref.at[span(d, g)] if s == 0 else gbuf.at[s - 1, span(d, g)]
        return pltpu.make_async_remote_copy(
            src_ref=src,
            dst_ref=gbuf.at[s, span(d, g)],
            send_sem=ag_ss.at[s, d, g],
            recv_sem=ag_sr.at[s, d, g],
            device_id={"head": right if d == 0 else left},
            device_id_type=MESH,
        )

    for g in range(SUB):
        for d in range(2):
            ag_copy(0, d, g).start()
    for b in range(n):
        wi_copy(b).start()

    @pl.when(ctx == 0)
    def _():
        s_in[...] = jnp.zeros_like(s_in)

    @pl.when(ctx == nctx - 1)
    def _():
        g_in[...] = jnp.zeros_like(g_in)

    first = lax.broadcasted_iota(jnp.int32, (q, q), 0)
    second = lax.broadcasted_iota(jnp.int32, (q, q), 1)
    low = lax.broadcasted_iota(jnp.int32, (q, 2 * hp), 1) < hp

    def scaled(factor, state):
        out = factor[:, None, :] * state.reshape(heads, hp, nstate)
        return out.reshape(width, nstate)

    hstep = heads // PIECES
    step = width // PIECES

    def relay(own, got, out, sends, recvs, target, receives, passes):
        def copy(i):
            at = pl.ds(i * step, step)
            return pltpu.make_async_remote_copy(
                src_ref=out.at[at],
                dst_ref=got.at[at],
                send_sem=sends.at[i],
                recv_sem=recvs.at[i],
                device_id={"ctx": target},
                device_id_type=MESH,
            )

        def run():
            for i in range(PIECES):
                at = pl.ds(i * step, step)

                @pl.when(receives)
                def _():
                    copy(i).wait_recv()

                @pl.when(passes)
                def _():
                    factor = etot[nc, i * hstep : (i + 1) * hstep, :]
                    come = got[at, :].astype(F32).reshape(hstep, hp, nstate)
                    come = (factor[:, None, :] * come).reshape(step, nstate)
                    out[at, :] = (own[at, :] + come).astype(BF16)
                    copy(i).start()

        def finish():
            @pl.when(passes)
            def _():
                for i in range(PIECES):
                    copy(i).wait_send()

        return run, finish

    run_s, finish_s = relay(
        end_own, s_in, s_out, st_ss, st_sr, ahead, ctx > 0, ctx < nctx - 1
    )
    run_g, finish_g = relay(
        leave_own, g_in, g_out, gr_ss, gr_sr, behind, ctx < nctx - 1, ctx > 0
    )

    x_copy().wait()
    upto = (first <= second).astype(F32)
    downto = (first >= second).astype(F32)
    after = (first < second).astype(F32)
    ones = jnp.ones((q, nstate), F32)
    head_at = lax.broadcasted_iota(jnp.int32, (heads, width), 0) * hp
    lane_at = lax.broadcasted_iota(jnp.int32, (heads, width), 1)
    spread = ((lane_at >= head_at) & (lane_at < head_at + hp)).astype(BF16)
    total = jnp.zeros((heads, nstate), F32)
    for k in range(nc):
        at = pl.ds(k * q, q)
        ldk = ld_ref[:, k * q : (k + 1) * q]
        lrow[k] = mm(ldk, upto, precision=HIGH)
        lc = mm(downto, ldk, NT, HIGH)
        lcol[k] = lc
        whole = mm(ldk, ones, precision=HIGH)
        total = total + whole
        etot[k] = jnp.exp(whole)
        fade = mm(jnp.exp(mm(after, ldk, NT, HIGH)).astype(BF16), spread)
        fades[at, :] = fade.astype(BF16)
        grows[at, :] = mm(jnp.exp(lc).astype(BF16), spread).astype(BF16)
        fx = (xv[at, :].astype(F32) * fade).astype(BF16)
        faded[at, :] = fx
        ends[k] = mm(fx, b_ref[at, :], TN)
    etot[nc] = jnp.exp(total)
    state = ends[0]
    for k in range(1, nc):
        state = scaled(etot[k], state) + ends[k]
    end_own[...] = state

    def prepare(k):
        at = pl.ds(pl.multiple_of(k * q, q), q)
        score = mm(b_ref[at, :], c_ref[at, :], NT)
        score2 = jnp.concatenate([score, score], axis=1)
        keep = jnp.concatenate([first <= second, first <= second], axis=1)
        colk = lcol[k]
        for j in range(pairs):
            d0 = lrow[k, 2 * j : 2 * j + 1, :] - colk[:, 2 * j : 2 * j + 1]
            d1 = lrow[k, 2 * j + 1 : 2 * j + 2, :] - colk[:, 2 * j + 1 : 2 * j + 2]
            decay = jnp.exp(jnp.where(keep, jnp.concatenate([d0, d1], axis=1), -1e30))
            decays[k, j] = decay
            mixes[k, j] = (decay * score2).astype(BF16)

    def owner(s, d):
        return ring_index(lax.rem(place + (n - s if d == 0 else s), n), n)

    def accumulate(s, d, row0, count):
        own = owner(s, d)
        src = grad_ref if s == 0 else gbuf.at[s - 1]

        @pl.loop(0, width // TILE)
        def _(j):
            lanes = pl.ds(pl.multiple_of(j * TILE, TILE), TILE)
            part = mm(src[pl.ds(row0, count), :], wo[own, lanes, :], NT)
            at = (pl.ds(row0, count), lanes)
            if s == 0:
                acc[at] = part
            elif s == n - 1:
                dy[at] = (acc[at] + part).astype(dy.dtype)
            else:
                acc[at] += part

    for b in range(n):
        wo_copy(b).wait()
    at_s = (ctx * (n - 1)) // nctx
    for s in range(n - 1):
        if s > 0:
            for g in range(SUB):
                for d in range(2):
                    ag_copy(s - 1, d, g).wait_recv()
                    ag_copy(s, d, g).start()
        for d in range(2):
            accumulate(s, d, d * half, half)
        pl.when(at_s == s)(run_s)
        if s > 0:
            lo, hi = (nc * (s - 1)) // (n - 2), (nc * s) // (n - 2)
            if hi > lo:
                pl.loop(lo, hi)(prepare)
    for g in range(SUB):
        for d in range(2):
            ag_copy(n - 2, d, g).wait_recv()
            accumulate(n - 1, d, d * half + g * piece, piece)

    for k in range(nc):
        at = pl.ds(k * q, q)
        gd = dy[at, :] * grows[at, :]
        grown[at, :] = gd
        leaves[k] = mm(gd, c_ref[at, :], TN)
    grad = leaves[nc - 1]
    for k in range(nc - 2, -1, -1):
        grad = leaves[k] + scaled(etot[k], grad)
    leave_own[...] = grad

    points = POINTS * nc
    at_g = ((nctx - 1 - ctx) * points) // nctx

    @pl.loop(0, nc)
    def _(k):
        at = pl.ds(pl.multiple_of(k * q, q), q)
        for j in range(pairs):
            if j % (pairs // POINTS) == 0:
                pl.when(k * POINTS + j // (pairs // POINTS) == at_g)(run_g)
            lanes = slice(j * 2 * hp, (j + 1) * 2 * hp)
            dyp = dy[at, lanes]
            none = jnp.zeros_like(dyp)
            dyst = jnp.concatenate([jnp.where(low, dyp, none), jnp.where(low, none, dyp)], axis=0)
            mixed = decays[k, j] * mm(xv[at, lanes], dyst, NT)
            if j == 0:
                wacc[...] = mixed
            else:
                wacc[...] += mixed
            intra[at, lanes] = mm(mixes[k, j], dyst)
        both = wacc[...]
        weight = (both[:, :q] + both[:, q:]).astype(BF16)
        wg_ref[at, :] = mm(weight, c_ref[at, :])
        rg_ref[at, :] = mm(weight, b_ref[at, :], TN)

    state = s_in[...].astype(F32)
    for k in range(nc):
        at = pl.ds(k * q, q)
        rg_ref[at, :] += mm(grown[at, :], state.astype(BF16))
        if k < nc - 1:
            state = scaled(etot[k], state) + ends[k]
    for b in range(n):
        wi_copy(b).wait()
    grad = g_in[...].astype(F32)
    for k in range(nc - 1, -1, -1):
        at = pl.ds(k * q, q)
        gb = grad.astype(BF16)
        inter = mm(b_ref[at, :], gb, NT)
        xg[at, :] = (intra[at, :] + fades[at, :].astype(F32) * inter).astype(BF16)
        wg_ref[at, :] += mm(faded[at, :], gb)
        if k > 0:
            grad = leaves[k] + scaled(etot[k], grad)

    def rs_copy(s, d, g):
        return pltpu.make_async_remote_copy(
            src_ref=sbuf.at[s, span(d, g)],
            dst_ref=rbuf.at[s, span(d, g)],
            send_sem=rs_ss.at[s, d, g],
            recv_sem=rs_sr.at[s, d, g],
            device_id={"head": right if d == 0 else left},
            device_id_type=MESH,
        )

    def term(s, d, row0, count, dest_ref):
        if d == 0:
            dest = ring_index(lax.rem(place + 2 * n - 1 - s, n), n)
        else:
            dest = ring_index(lax.rem(place + 1 + s, n), n)
        at = pl.ds(row0, count)

        @pl.loop(0, cols // TILE)
        def _(j):
            lanes = pl.ds(pl.multiple_of(j * TILE, TILE), TILE)
            part = mm(xg[at, :], wi[dest, lanes, :], NT)
            dest_ref[at, lanes] = part.astype(dest_ref.dtype)

    for g in range(SUB):
        for d in range(2):
            term(0, d, d * half + g * piece, piece, sbuf.at[0])
            rs_copy(0, d, g).start()
    for s in range(1, n):
        for d in range(2):
            term(s, d, d * half, half, acc)
        for g in range(SUB):
            for d in range(2):
                rs_copy(s - 1, d, g).wait_recv()
                at = span(d, g)
                part = acc[at, :cols] + rbuf[s - 1, at, :].astype(F32)
                if s == n - 1:
                    out_ref[at, :] = part.astype(out_ref.dtype)
                else:
                    sbuf[s, at, :] = part.astype(BF16)
                    rs_copy(s, d, g).start()
    for s in range(n - 1):
        for g in range(SUB):
            for d in range(2):
                ag_copy(s, d, g).wait_send()
                rs_copy(s, d, g).wait_send()
    finish_s()
    finish_g()


def per_device(
    nctx, nhead, ssd_input, log_decay, write_proj, read_proj, in_weight, out_weight, out_grad
):
    rows, width = ssd_input.shape
    nstate = write_proj.shape[2]
    heads = log_decay.shape[0]
    feats = out_grad.shape[1]
    n = nhead
    cols = in_weight.shape[0] // n
    nc = rows // CHUNK
    pairs = heads // 2
    vm = pl.BlockSpec(memory_space=pltpu.VMEM)
    hbm = pl.BlockSpec(memory_space=pl.ANY)
    dma = pltpu.SemaphoreType.DMA
    state = pltpu.VMEM((width, nstate), BF16)
    input_grad, write_grad, read_grad = pl.pallas_call(
        functools.partial(layer_kernel, nctx, nhead),
        name="layer",
        out_shape=(
            jax.ShapeDtypeStruct((rows, cols), BF16),
            jax.ShapeDtypeStruct((rows, nstate), F32),
            jax.ShapeDtypeStruct((rows, nstate), F32),
        ),
        in_specs=[vm, hbm, vm, vm, vm, hbm, hbm],
        out_specs=(vm, vm, vm),
        scratch_shapes=[
            pltpu.VMEM((rows, width), BF16),
            pltpu.VMEM((rows, width), BF16),
            pltpu.VMEM((rows, width), BF16),
            pltpu.VMEM((n, width, feats), BF16),
            pltpu.VMEM((n, cols, width), BF16),
            pltpu.VMEM((rows, max(width, cols)), F32),
            pltpu.VMEM((n - 1, rows, feats), BF16),
            pltpu.VMEM((n - 1, rows, cols), BF16),
            pltpu.VMEM((n - 1, rows, cols), BF16),
            pltpu.VMEM((nc, width, nstate), F32),
            pltpu.VMEM((nc, width, nstate), F32),
            pltpu.VMEM((rows, width), BF16),
            pltpu.VMEM((rows, width), BF16),
            pltpu.VMEM((rows, width), BF16),
            pltpu.VMEM((rows, width), BF16),
            pltpu.VMEM((rows, width), F32),
            pltpu.VMEM((nc, pairs, CHUNK, 2 * CHUNK), F32),
            pltpu.VMEM((nc, pairs, CHUNK, 2 * CHUNK), BF16),
            pltpu.VMEM((nc, heads, CHUNK), F32),
            pltpu.VMEM((nc, CHUNK, heads), F32),
            pltpu.VMEM((nc + 1, heads, nstate), F32),
            pltpu.VMEM((CHUNK, 2 * CHUNK), F32),
            pltpu.VMEM((width, nstate), F32),
            pltpu.VMEM((width, nstate), F32),
            state, state, state, state,
            dma, dma((n,)), dma((n,)),
            dma((n - 1, 2, SUB)), dma((n - 1, 2, SUB)),
            dma((n - 1, 2, SUB)), dma((n - 1, 2, SUB)),
            dma((PIECES,)), dma((PIECES,)), dma((PIECES,)), dma((PIECES,)),
        ],
        compiler_params=pltpu.CompilerParams(
            collective_id=0, has_side_effects=True, vmem_limit_bytes=VMEM_LIMIT
        ),
    )(
        out_grad,
        ssd_input,
        log_decay,
        write_proj.reshape(rows, nstate),
        read_proj.reshape(rows, nstate),
        out_weight,
        in_weight,
    )
    return (input_grad, write_grad.reshape(rows, 1, nstate), read_grad.reshape(rows, 1, nstate))


def solution(mesh):
    placed = (
        P("ctx", "head"),
        P("head", "ctx"),
        P("ctx", "head", None),
        P("ctx", "head", None),
        P(None, "head"),
        P("head", None),
        P("ctx", "head"),
    )
    return jax.shard_map(
        functools.partial(per_device, mesh.shape["ctx"], mesh.shape["head"]),
        mesh=mesh,
        in_specs=placed,
        out_specs=(P("ctx", "head"), P("ctx", "head", None), P("ctx", "head", None)),
        check_vma=False,
    )
```

time: 273 us -> 106 us (0.39)
  waiting for transfers between devices: 110 us -> 0 us
  Pallas kernels: 0 us -> 99.5 us
  matrix products: 68.2 us -> 0 us
  local copies, waits for them, and re-layouts: 41.1 us -> 5.6 us
  other arithmetic: 20.3 us -> 0 us
  blocking collectives: 17.1 us -> 0 us
  between operations: 14.7 us -> 0.64 us
    pallas_call x0 -> x1, Pallas kernels: none -> 99.5 us  [per_device(): pl.pallas_call(functools.partial(layer_kernel, nctx, nhead), name='layer'...]
    dot_general x25 -> x0, matrix products: 68.2 us -> none  [the longest x1 9.79 us: per_device(): lax.dot_general(x_grad, in_weight, (((1,), (1,)), ((), ())), preferred_el...]
    all_gather x3 -> x0, waiting for transfers between devices: 62.7 us -> none  [the longest x1 52.1 us: per_device(): lax.all_gather(out_grad, 'head', axis=1, tiled=True)]
    reduce_scatter x1 -> x0, waiting for transfers between devices: 46.2 us -> none  [per_device(): lax.psum_scatter(terms.astype(jnp.bfloat16), 'head', scatter_dimension=1,...]
    unnamed x1 -> x0, blocking collectives: 17.1 us -> none
    reshape x7 -> x0, local copies, waits for them, and re-layouts: 7.09 us -> none  [the longest x3 3.68 us: head_rows(): return jnp.repeat(per_head.T, head_size, axis=1)]
    another operation x10 -> x0, local copies, waits for them, and re-layouts: 5.58 us -> none
    dynamic_update_slice x4 -> x0, local copies, waits for them, and re-layouts: 5.32 us -> none  [per_device(): lax.scan(forward_stretch, zeros, (xs, dys, write_blocks, read_blocks, str...]
  transfers between devices with their start and end apart: 4 -> 0, of which waited for: 4 -> 0; matrix products, arithmetic and copies ran while one was open for 16% -> 0% of each run, Pallas kernels for 0% -> 0%
where the time goes in v2:
time: 106 us
  Pallas kernels  99.5 us (94%)
  local copies, waits for them, and re-layouts  5.6 us (5%)
    pallas_call x1, Pallas kernels, per_device(): pl.pallas_call(functools.partial(layer_kernel, nctx, nhead), name='layer'...  99.5 us
    unnamed x3, local copies, waits for them, and re-layouts  5.6 us

profile of v2, /device:TPU:0, one launch (start us, length us, event | category | flops | bytes accessed | tf_op | source)
XLA Modules:
  0.0 105.7 jit_solution(5452189247786435529)
XLA Ops:
  0.6 99.5 %layer.1 = (bf16[512,1024]{1,0:T(8,128)(2,1)}, f32[512,128]{1,0:T(8,128)}, f32[512,128]{1,0:T(8,128)}) custom-call(bf16[512,1024]{1,0:T(8,128)(2,1)} %grad_ref.1, bf16[512,1024]{1,0:T(8,128)(2,1)} %x_hbm.1, f32[16,512]{1,0:T(8,128)} %ld_ref.1, bf16[512,128]{1,0:T(8,128)(2,1)} %bitcast.10, bf16[512,128]{1,0:T(8,128)(2,1)} %bitcast.11, ...), custom_call_target="tpu_custom_call" | custom-call | tf_op jit(solution)/shard_map/layer/pallas_call | solution.py:373
  100.1 2.3 %copy.15 = bf16[512,1024]{1,0:T(8,128)(2,1)} copy(bf16[512,1024]{1,0:T(8,128)(2,1)} %get-tuple-element.15) | data formatting | bytes 2097152
  102.4 1.7 %copy.16 = f32[512,1,128]{2,1,0:T(1,128)} copy(f32[512,1,128]{2,1,0:T(1,128)} %bitcast.9) | data formatting | bytes 524288
  104.0 1.7 %copy.17 = f32[512,1,128]{2,1,0:T(1,128)} copy(f32[512,1,128]{2,1,0:T(1,128)} %bitcast.8) | data formatting | bytes 524288

commit v3 on v2

--- a/solution.py
+++ b/solution.py
@@ -9,7 +9,7 @@
 
 CHUNK = 128
 SUB = 2
-PIECES = 4
+PIECES = 8
 POINTS = 2
 TILE = 256
 MESH = pl.DeviceIdType.MESH
@@ -288,12 +288,6 @@
         wg_ref[at, :] = mm(weight, c_ref[at, :])
         rg_ref[at, :] = mm(weight, b_ref[at, :], TN)
 
-    state = s_in[...].astype(F32)
-    for k in range(nc):
-        at = pl.ds(k * q, q)
-        rg_ref[at, :] += mm(grown[at, :], state.astype(BF16))
-        if k < nc - 1:
-            state = scaled(etot[k], state) + ends[k]
     for b in range(n):
         wi_copy(b).wait()
     grad = g_in[...].astype(F32)
@@ -333,6 +327,12 @@
         for d in range(2):
             term(0, d, d * half + g * piece, piece, sbuf.at[0])
             rs_copy(0, d, g).start()
+    state = s_in[...].astype(F32)
+    for k in range(nc):
+        at = pl.ds(k * q, q)
+        rg_ref[at, :] += mm(grown[at, :], state.astype(BF16))
+        if k < nc - 1:
+            state = scaled(etot[k], state) + ends[k]
     for s in range(1, n):
         for d in range(2):
             term(s, d, d * half, half, acc)

time: 106 us -> 105 us (level)
  Pallas kernels: 99.5 us -> 98.3 us
    pallas_call x1, Pallas kernels: 99.5 us -> 98.3 us  [per_device(): pl.pallas_call(functools.partial(layer_kernel, nctx, nhead), name='layer'...]
where the time goes in v3:
time: 105 us
  Pallas kernels  98.3 us (94%)
  local copies, waits for them, and re-layouts  5.6 us (5%)
    pallas_call x1, Pallas kernels, per_device(): pl.pallas_call(functools.partial(layer_kernel, nctx, nhead), name='layer'...  98.3 us
    unnamed x3, local copies, waits for them, and re-layouts  5.6 us

profile of v3, /device:TPU:0, one launch (start us, length us, event | category | flops | bytes accessed | tf_op | source)
XLA Modules:
  0.0 104.5 jit_solution(4848827964769313986)
XLA Ops:
  0.6 98.3 %layer.1 = (bf16[512,1024]{1,0:T(8,128)(2,1)}, f32[512,128]{1,0:T(8,128)}, f32[512,128]{1,0:T(8,128)}) custom-call(bf16[512,1024]{1,0:T(8,128)(2,1)} %grad_ref.1, bf16[512,1024]{1,0:T(8,128)(2,1)} %x_hbm.1, f32[16,512]{1,0:T(8,128)} %ld_ref.1, bf16[512,128]{1,0:T(8,128)(2,1)} %bitcast.10, bf16[512,128]{1,0:T(8,128)(2,1)} %bitcast.11, ...), custom_call_target="tpu_custom_call" | custom-call | tf_op jit(solution)/shard_map/layer/pallas_call | solution.py:373
  98.9 2.3 %copy.15 = bf16[512,1024]{1,0:T(8,128)(2,1)} copy(bf16[512,1024]{1,0:T(8,128)(2,1)} %get-tuple-element.15) | data formatting | bytes 2097152
  101.2 1.7 %copy.16 = f32[512,1,128]{2,1,0:T(1,128)} copy(f32[512,1,128]{2,1,0:T(1,128)} %bitcast.9) | data formatting | bytes 524288
  102.9 1.7 %copy.17 = f32[512,1,128]{2,1,0:T(1,128)} copy(f32[512,1,128]{2,1,0:T(1,128)} %bitcast.8) | data formatting | bytes 524288
